TPU v7x, 512 devices: a whole 4x4x16 slice. The times are simulated.
512 devices in a mesh: dp: 8 (over y_hi, x), tile: 64 (over y_lo, z, core).
Axes of the slice: x: 4, y: 4 (y_hi: 2, y_lo: 2; y = y_hi * 2 + y_lo), z: 16, core: 2. Of those that a mesh axis runs over, the one named last changes fastest.
Arguments:
- ocean_state: bfloat16 [8, 256, 64, 768], P('dp', 'tile'), may hold values from -6 to 6
- cotangent: bfloat16 [8, 256, 64, 768], P('dp', 'tile'), may hold values from -6 to 6
- depth_kernel: float32 [7, 7, 768], replicated, may hold values from -0.875 to 0.875
- norm_gain: float32 [768], replicated, may hold values from 0.5 to 2
- expand_weight: bfloat16 [768, 3072], P('tile'), may hold values from -0.21875 to 0.21875
- expand_bias: float32 [3072], replicated, may hold values from -4 to 4
- reduce_weight: bfloat16 [3072, 768], P('tile'), may hold values from -0.109375 to 0.109375
- tile_slot: int32 [256], P('tile'), may hold values from -1 to 5, as said below
Outputs:
- state_grad: bfloat16 [8, 256, 64, 768], P('dp', 'tile')
- kernel_grad: float32 [7, 7, 768], replicated
- gain_grad: float32 [768], replicated
- bias_grad: float32 [3072], replicated
Inputs may be any that keep to these rules, and one draw needn't show every extreme that they name: `tile_slot`: entry t is -1 for a land tile, k < 3 for slot k of the tile's own device, 3 + k for slot k of the device whose tile index differs by half of the axis; the tiles of a device and of that device together name each slot of either at most once, and on some pair of devices every slot is named.
All inputs are finite; a program needn't handle non-finite values.
Results may differ from a plain program's by a relative error of at most 0.0085.
Values may be sent and summed in bfloat16 or wider, within the bound.
No kernel may reach another device: no remote copies, remote signals or barrier semaphores. Data moves between devices by JAX's collectives and lax.ppermute only.
A program may use at most 64 MiB of HBM per device.

v0:
```python
import math
import jax
import jax.numpy as jnp
from jax import lax
from jax.sharding import PartitionSpec as P

KS = 7


def with_halo(cells, sides, width):
    for axis, dim in sides:
        count = lax.axis_size(axis)
        ends = count - 1
        head = lax.slice_in_dim(cells, 0, width, axis=dim)
        tail = lax.slice_in_dim(cells, cells.shape[dim] - width, cells.shape[dim], axis=dim)
        cells = jnp.concatenate(
            [
                lax.ppermute(tail, axis, [(i, (i + 1) % count) for i in range(ends)]),
                cells,
                lax.ppermute(head, axis, [((i + 1) % count, i) for i in range(ends)]),
            ],
            axis=dim,
        )
    return cells


def depthwise(padded, kernel, row_count, col_count):
    total = None
    for shift_row in range(KS):
        band = padded[..., shift_row : shift_row + row_count, :, :]
        part = kernel[shift_row, 0] * band[..., 0:col_count, :].astype(jnp.float32)
        for shift_col in range(1, KS):
            part = part + kernel[shift_row, shift_col] * band[
                ..., shift_col : shift_col + col_count, :
            ].astype(jnp.float32)
        total = part if total is None else total + part
    return total


def gelu_slope(value):
    factor = math.sqrt(2.0 / math.pi)
    inner = factor * (value + 0.044715 * value * value * value)
    tangent = jnp.tanh(inner)
    return 0.5 * (1.0 + tangent) + 0.5 * value * (1.0 - tangent * tangent) * factor * (
        1.0 + 3.0 * 0.044715 * value * value
    )


def local(
    ocean_state,
    cotangent,
    depth_kernel,
    norm_gain,
    expand_weight,
    expand_bias,
    reduce_weight,
    tile_slot,
):
    samples, row_count, col_count, channels = ocean_state.shape
    tile_count = tile_slot.shape[0]
    tile_rows = row_count // tile_count
    rim = KS // 2
    padded = with_halo(ocean_state, (("tile", 1),), rim)
    padded = jnp.pad(padded, ((0, 0), (0, 0), (rim, rim), (0, 0)))
    mixed = depthwise(padded, depth_kernel, row_count, col_count)
    centred = mixed - jnp.mean(mixed, axis=-1, keepdims=True)
    inverse = lax.rsqrt(jnp.mean(centred * centred, axis=-1, keepdims=True) + 1e-06)
    normed = centred * inverse
    scaled = (normed * norm_gain).astype(jnp.bfloat16)
    row_mask = jnp.repeat(tile_slot >= 0, tile_rows).astype(jnp.bfloat16)
    masked = cotangent * row_mask[None, :, None, None]
    contract_last = (((1,), (1,)), ((), ()))
    full_expand, full_reduce = (
        lax.all_gather(expand_weight, "tile", axis=0, tiled=True),
        lax.all_gather(reduce_weight, "tile", axis=0, tiled=True),
    )
    hidden = (
        jnp.dot(scaled.reshape(-1, channels), full_expand, preferred_element_type=jnp.float32)
        + expand_bias
    )
    back_act = lax.dot_general(
        masked.reshape(-1, channels), full_reduce, contract_last, preferred_element_type=jnp.float32
    )
    back_hidden = (back_act * gelu_slope(hidden)).astype(jnp.bfloat16)
    back_scaled = lax.dot_general(
        back_hidden, full_expand, contract_last, preferred_element_type=jnp.float32
    ).astype(jnp.bfloat16)
    scaled_back = back_scaled
    bias_part = jnp.sum(back_hidden.astype(jnp.float32), axis=0)
    back_scaled = scaled_back.reshape(samples, row_count, col_count, channels)
    back_float = back_scaled.astype(jnp.float32)
    gain_part = jnp.sum(back_float * normed, axis=(0, 1, 2))
    back_norm = back_float * norm_gain
    back_mixed = inverse * (
        back_norm
        - jnp.mean(back_norm, axis=-1, keepdims=True)
        - normed * jnp.mean(back_norm * normed, axis=-1, keepdims=True)
    )
    back_mixed = back_mixed.astype(jnp.bfloat16)
    mixed_float = back_mixed.astype(jnp.float32)
    kernel_rows = []
    for shift_row in range(KS):
        band = padded[:, shift_row : shift_row + row_count, :, :]
        kernel_cols = [
            jnp.sum(
                band[:, :, shift_col : shift_col + col_count, :].astype(jnp.float32) * mixed_float,
                axis=(0, 1, 2),
            )
            for shift_col in range(KS)
        ]
        kernel_rows.append(jnp.stack(kernel_cols))
    kernel_part = jnp.stack(kernel_rows)
    back_padded = with_halo(back_mixed, (("tile", 1),), rim)
    back_padded = jnp.pad(back_padded, ((0, 0), (0, 0), (rim, rim), (0, 0)))
    through = depthwise(back_padded, depth_kernel[::-1, ::-1], row_count, col_count)
    state_grad = (cotangent.astype(jnp.float32) + through).astype(jnp.bfloat16)
    kernel_grad, gain_grad, bias_grad = lax.psum(
        (kernel_part, gain_part, bias_part), ("dp", "tile")
    )
    return (state_grad, kernel_grad, gain_grad, bias_grad)


def solution(mesh):
    return jax.shard_map(
        local,
        mesh=mesh,
        in_specs=(
            P("dp", "tile", None, None),
            P("dp", "tile", None, None),
            P(),
            P(),
            P("tile", None),
            P(),
            P("tile", None),
            P("tile"),
        ),
        out_specs=(P("dp", "tile", None, None), P(), P(), P()),
        check_vma=False,
    )
```

profile of v0, /device:TPU:1, one launch (start us, length us, event | category | flops | bytes accessed | tf_op | source)
XLA Modules:
  0.0 757.2 jit_solution(15072238544217701571)
XLA Ops:
  7.2 0.0 copy-start
  7.2 0.0 copy-start.8
  7.2 0.0 all-gather.6.cloned.1.call-start
  7.2 0.7 all-gather.6.cloned.1.call-update
  7.9 0.0 all-gather.4.cloned.1.call-start
  8.0 0.7 all-gather.4.cloned.1.call-update
  8.7 0.0 all-reduce.5.cloned.1.call-start
  8.7 1.1 fusion.127
  9.8 4.9 collective-permute-start
  14.7 5.1 collective-permute-start.1
  19.9 0.7 compare_convert_fusion
  20.5 1.9 broadcast_multiply_fusion
  22.4 1.4 slice_reduce_fusion.48
  23.8 0.0 copy-done.8
  23.8 0.2 slice_reduce_fusion.47
  24.0 0.1 slice_reduce_fusion.46
  24.1 0.0 copy-start.10
  24.1 0.0 collective-permute-done
  24.2 0.1 constant_dynamic-update-slice_fusion
  24.2 0.0 copy-start.1
  24.2 0.0 collective-permute-done.1
  24.3 0.3 fusion.12
  24.6 0.1 copy-done.10
  24.7 0.0 copy-done.12
  24.7 0.0 copy-done.14
  24.7 0.0 copy-done.16
  24.7 0.0 copy-done.18
  24.7 6.4 fusion.124
  31.1 0.2 multiply_reduce_fusion.3
  31.4 0.0 copy-done.9
  31.4 0.0 copy-start.20
  31.4 0.9 multiply_convert_fusion.1
  32.3 109.8 %all-gather.6.cloned.1.call-done = bf16[64,12,3072]{2,1,0:T(8,128)(2,1)} async-done(((bf16[1,12,3072]{2,1,0:T(8,128)(2,1)}), bf16[64,12,3072]{2,1,0:T(8,128)(2,1)}) %all-gather.6.cloned.1.call-update) | async-done | bytes 4718608 | tf_op jit(solution)/shard_map/all_gather | solution.py:74
  142.1 7.5 reshape.394
  149.6 0.0 copy-done.20
  149.6 5.5 convolution_add_fusion
  155.2 109.3 %all-gather.4.cloned.1.call-done = bf16[3072,768]{1,0:T(8,128)(2,1)} async-done(((bf16[48,768]{1,0:T(8,128)(2,1)}), bf16[3072,768]{1,0:T(8,128)(2,1)}) %all-gather.4.cloned.1.call-update) | async-done | bytes 4718608 | tf_op jit(solution)/shard_map/all_gather | solution.py:75
  264.5 7.3 convert_reduce_fusion
  271.8 2.3 multiply_reduce_fusion.2
  274.1 0.7 div.17
  274.7 0.0 copy-done.21
  274.7 2.4 multiply_reduce_fusion
  277.1 0.0 copy-done.3
  277.1 3.7 fusion.118
  280.9 0.0 copy-done.2
  280.9 1.2 fusion.117
  282.0 0.0 copy-start.23
  282.0 0.0 copy-start.22
  282.1 2.0 fusion.119
  284.1 0.0 copy-start.24
  284.1 0.0 copy-start.25
  284.1 0.0 copy-start.5
  284.8 3.3 collective-permute-start.2
  288.1 2.1 collective-permute-start.3
  290.7 0.0 copy-start.7
  290.7 0.7 copy-done.7
  291.4 0.0 all-reduce.5.cloned.1.call-update
  291.4 102.4 %all-reduce.2 = (f32[768]{0:T(1024)}, f32[3072]{0:T(1024)}) all-reduce(f32[768]{0:T(1024)S(1)} %copy-done.24, f32[3072]{0:T(1024)S(1)} %copy-done.25), channel_id=1, replica_groups=mesh['dp'=8,'tile'=64] {'dp','tile'}, use_global_device_ids=true, to_apply=%region_55.56 | all-reduce | flops 3840 | bytes 30720 | tf_op jit(solution)/shard_map/psum | solution.py:117
  393.8 0.0 collective-permute-done.2
  393.8 0.0 collective-permute-done.3
  393.8 0.3 select_maximum_fusion
  394.2 6.5 fusion.70
  400.7 348.3 %all-reduce.5.cloned.1.call-done = f32[7,7,768]{2,1,0:T(8,128)} async-done(((f32[7,7,768]{2,1,0:T(8,128)}), f32[7,7,768]{2,1,0:T(8,128)}) %all-reduce.5.cloned.1.call-update) | async-done | bytes 150544 | tf_op jit(solution)/shard_map/psum | solution.py:117
  749.0 1.6 copy.21
  (101 shorter events, 0.7 us)
Async XLA Ops:
  7.2 17.0 %copy-start = (bf16[1,4,64,768]{3,2,1,0:T(8,128)(2,1)S(1)}, bf16[1,4,64,768]{3,2,1,0:T(8,128)(2,1)}, u32[]{:S(2)}) copy-start(bf16[1,4,64,768]{3,2,1,0:T(8,128)(2,1)} %param.8) | copy-start | bytes 1179652
  7.2 16.6 %copy-start.8 = (f32[7,7,768]{2,1,0:T(8,128)S(1)}, f32[7,7,768]{2,1,0:T(8,128)}, u32[]{:S(2)}) copy-start(f32[7,7,768]{2,1,0:T(8,128)} %param.10) | copy-start | bytes 451588
  7.2 134.9 %all-gather.6.cloned.1.call-start = ((), (), s32[]{:S(2)}) async-start(), calls=%async_computation.2 | async-start | bytes 6389760 | tf_op jit(solution)/shard_map/all_gather | solution.py:74
  7.9 256.6 %all-gather.4.cloned.1.call-start = ((), (), s32[]{:S(2)}) async-start(), calls=%async_computation | async-start | bytes 4792320 | tf_op jit(solution)/shard_map/all_gather | solution.py:75
  8.7 740.4 %all-reduce.5.cloned.1.call-start = ((), (), s32[]{:S(2)}) async-start(), calls=%async_computation.1 | async-start | bytes 344064 | tf_op jit(solution)/shard_map/psum | solution.py:117
  9.8 14.3 %collective-permute-start = (bf16[1,3,64,768]{3,2,1,0:T(8,128)(2,1)S(1)}, bf16[1,3,64,768]{3,2,1,0:T(8,128)(2,1)S(1)}, u32[]{:S(2)}, u32[]{:S(2)}) collective-permute-start(bf16[1,3,64,768]{3,2,1,0:T(8,128)(2,1)S(1)} %get-tuple-element.119), channel_id=1, source_target_pairs={{0,1},{1,2},{2,3},{3,4},{4,5},{5,6},{6,7},{7,8},{8,9},{9,10},{10,1... | collective-permute-start | bytes 884744 | tf_op jit(solution)/shard_map/ppermute | solution.py:18
  14.7 9.5 %collective-permute-start.1 = (bf16[1,3,64,768]{3,2,1,0:T(8,128)(2,1)S(1)}, bf16[1,3,64,768]{3,2,1,0:T(8,128)(2,1)S(1)}, u32[]{:S(2)}, u32[]{:S(2)}) collective-permute-start(bf16[1,3,64,768]{3,2,1,0:T(8,128)(2,1)S(1)} %get-tuple-element.120), channel_id=1, source_target_pairs={{1,0},{2,1},{3,2},{4,3},{5,4},{6,5},{7,6},{8,7},{9,8},{10,9},{11,1... | collective-permute-start | bytes 884744 | tf_op jit(solution)/shard_map/ppermute | solution.py:20
  24.1 0.6 copy-start.10
  24.1 0.6 copy-start.12
  24.1 0.6 copy-start.14
  24.1 0.6 copy-start.16
  24.1 0.6 copy-start.18
  24.2 6.9 copy-start.1
  24.7 6.7 copy-start.9
  31.4 118.3 %copy-start.20 = (f32[4,64]{1,0:T(4,128)}, f32[4,64]{1,0:T(4,128)S(1)}, u32[]{:S(2)}) copy-start(f32[4,64]{1,0:T(4,128)S(1)} %add_rsqrt_fusion) | copy-start | bytes 3076
  149.6 114.8 %copy-start.6 = (bf16[1,4,64,768]{3,2,1,0:T(8,128)(2,1)S(1)}, bf16[1,4,64,768]{3,2,1,0:T(8,128)(2,1)}, u32[]{:S(2)}) copy-start(bf16[1,4,64,768]{3,2,1,0:T(8,128)(2,1)} %broadcast_multiply_fusion) | copy-start | bytes 1179652
  264.5 7.3 copy-start.4
  271.8 3.0 copy-start.21
  274.7 2.4 copy-start.3
  274.7 2.4 copy-start.26
  277.1 3.7 copy-start.2
  282.0 8.5 %copy-start.23 = (f32[768]{0:T(1024)S(1)}, f32[768]{0:T(1024)}, u32[]{:S(2)}) copy-start(f32[768]{0:T(1024)} %get-tuple-element.22) | copy-start | bytes 9220
  282.0 8.5 %copy-start.22 = (f32[768]{0:T(1024)S(1)}, f32[768]{0:T(1024)}, u32[]{:S(2)}) copy-start(f32[768]{0:T(1024)} %get-tuple-element.39) | copy-start | bytes 9220
  284.1 7.3 copy-start.24
  284.1 7.3 copy-start.25
  284.1 110.1 %copy-start.5 = (bf16[1,4,64,768]{3,2,1,0:T(8,128)(2,1)S(1)}, bf16[1,4,64,768]{3,2,1,0:T(8,128)(2,1)}, u32[]{:S(2)}) copy-start(bf16[1,4,64,768]{3,2,1,0:T(8,128)(2,1)} %param.9) | copy-start | bytes 1179652
  284.1 110.1 %copy-start.11 = (f32[768]{0:T(1024)S(1)}, f32[768]{0:T(1024)}, u32[]{:S(2)}) copy-start(f32[768]{0:T(1024)} %copy-done.10) | copy-start | bytes 9220
  284.1 110.1 %copy-start.13 = (f32[768]{0:T(1024)S(1)}, f32[768]{0:T(1024)}, u32[]{:S(2)}) copy-start(f32[768]{0:T(1024)} %copy-done.12) | copy-start | bytes 9220
  284.1 110.1 %copy-start.15 = (f32[768]{0:T(1024)S(1)}, f32[768]{0:T(1024)}, u32[]{:S(2)}) copy-start(f32[768]{0:T(1024)} %copy-done.14) | copy-start | bytes 9220
  284.1 110.1 %copy-start.17 = (f32[768]{0:T(1024)S(1)}, f32[768]{0:T(1024)}, u32[]{:S(2)}) copy-start(f32[768]{0:T(1024)} %copy-done.16) | copy-start | bytes 9220
  284.1 110.1 %copy-start.19 = (f32[768]{0:T(1024)S(1)}, f32[768]{0:T(1024)}, u32[]{:S(2)}) copy-start(f32[768]{0:T(1024)} %copy-done.18) | copy-start | bytes 9220
  284.8 109.1 %collective-permute-start.2 = (bf16[1,3,64,768]{3,2,1,0:T(8,128)(2,1)S(1)}, bf16[1,3,64,768]{3,2,1,0:T(8,128)(2,1)S(1)}, u32[]{:S(2)}, u32[]{:S(2)}) collective-permute-start(bf16[1,3,64,768]{3,2,1,0:T(8,128)(2,1)S(1)} %get-tuple-element.115), channel_id=1, source_target_pairs={{0,1},{1,2},{2,3},{3,4},{4,5},{5,6},{6,7},{7,8},{8,9},{9,10},{10,1... | collective-permute-start | bytes 884744 | tf_op jit(solution)/shard_map/ppermute | solution.py:18
  288.1 105.7 %collective-permute-start.3 = (bf16[1,3,64,768]{3,2,1,0:T(8,128)(2,1)S(1)}, bf16[1,3,64,768]{3,2,1,0:T(8,128)(2,1)S(1)}, u32[]{:S(2)}, u32[]{:S(2)}) collective-permute-start(bf16[1,3,64,768]{3,2,1,0:T(8,128)(2,1)S(1)} %get-tuple-element.116), channel_id=1, source_target_pairs={{1,0},{2,1},{3,2},{4,3},{5,4},{6,5},{7,6},{8,7},{9,8},{10,9},{11,1... | collective-permute-start | bytes 884744 | tf_op jit(solution)/shard_map/ppermute | solution.py:20
  290.7 0.7 copy-start.7
Sparse Core Ops, SparseCore 0:
  10.1 131.8 all-gather.5
  144.2 120.1 all-gather.3
  291.5 457.4 all-reduce.4
where the time goes:
time: 758 us; the launch traced here: 757 us
  waiting for transfers between devices  569 us (75%)
  blocking collectives  102 us (13%)
  other arithmetic  26.5 us (3%)
  starting transfers between devices  15.6 us (2%)
  matrix products  15.1 us (2%)
  between operations  14.6 us (2%)
  local copies, waits for them, and re-layouts  14.1 us (2%)
    psum x1, waiting for transfers between devices, local(): lax.psum((kernel_part, gain_part, bias_part), ('dp', 'tile'))  348 us
    all_gather x1, waiting for transfers between devices, local(): lax.all_gather(expand_weight, 'tile', axis=0, tiled=True)  110 us
    all_gather x1, waiting for transfers between devices, local(): lax.all_gather(reduce_weight, 'tile', axis=0, tiled=True)  109 us
    psum x1, blocking collectives, local(): lax.psum((kernel_part, gain_part, bias_part), ('dp', 'tile'))  102 us
  transfers between devices with their start and end apart: 7, of which 3 were waited for; matrix products, arithmetic and copies ran while one was open for 4% of the time, Pallas kernels for 0%

commit v1 on v0

--- a/solution.py
+++ b/solution.py
@@ -72,7 +72,9 @@
     contract_last = (((1,), (1,)), ((), ()))
     full_expand, full_reduce = (
         lax.all_gather(expand_weight, "tile", axis=0, tiled=True),
-        lax.all_gather(reduce_weight, "tile", axis=0, tiled=True),
+        jnp.concatenate(
+            lax.all_to_all(jnp.stack([reduce_weight] * lax.axis_size("tile")), "tile", 0, 0), axis=0
+        ),
     )
     hidden = (
         jnp.dot(scaled.reshape(-1, channels), full_expand, preferred_element_type=jnp.float32)

time: 758 us -> 787 us (1.038)
  starting transfers between devices: 15.6 us -> 28.5 us
  waiting for transfers between devices: 569 us -> 581 us
    ppermute x2, waiting for transfers between devices: 0.01 us -> 229 us  [with_halo(): lax.ppermute(tail, axis, [(i, (i + 1) % count) for i in range(ends)])]
    all_gather x1, waiting for transfers between devices: 110 us -> 0.19 us  [local(): lax.all_gather(expand_weight, 'tile', axis=0, tiled=True)]
    all_gather x1 -> x0, waiting for transfers between devices: 109 us -> none  [local(): lax.all_gather(reduce_weight, 'tile', axis=0, tiled=True)]
    all_to_all x0 -> x1, starting transfers between devices: none -> 18.5 us  [local(): lax.all_to_all(jnp.stack([reduce_weight] * lax.axis_size('tile')), 'tile'...]
  transfers between devices with their start and end apart: 7 -> 7, of which waited for: 3 -> 4; matrix products, arithmetic and copies ran while one was open for 4% -> 4% of each run, Pallas kernels for 0% -> 0%
where the time goes in v1:
time: 787 us
  waiting for transfers between devices  581 us (74%)
  blocking collectives  108 us (14%)
  starting transfers between devices  28.5 us (4%)
  other arithmetic  24.2 us (3%)
  local copies, waits for them, and re-layouts  16 us (2%)
  between operations  14.9 us (2%)
  matrix products  14.3 us (2%)
    psum x1, waiting for transfers between devices, local(): lax.psum((kernel_part, gain_part, bias_part), ('dp', 'tile'))  348 us
    ppermute x2, waiting for transfers between devices, with_halo(): lax.ppermute(tail, axis, [(i, (i + 1) % count) for i in range(ends)])  229 us
    psum x1, blocking collectives, local(): lax.psum((kernel_part, gain_part, bias_part), ('dp', 'tile'))  108 us
    all_to_all x1, starting transfers between devices, local(): lax.all_to_all(jnp.stack([reduce_weight] * lax.axis_size('tile')), 'tile'...  18.5 us
  transfers between devices with their start and end apart: 7, of which 4 were waited for; matrix products, arithmetic and copies ran while one was open for 4% of the time, Pallas kernels for 0%

profile of v1, /device:TPU:1, one launch (start us, length us, event | category | flops | bytes accessed | tf_op | source)
XLA Modules:
  0.0 786.5 jit_solution(16127299949530987927)
XLA Ops:
  7.2 3.4 stack.259
  10.6 18.5 %all-to-all-start = ((bf16[64,48,768]{2,1,0:T(8,128)(2,1)}), bf16[64,48,768]{2,1,0:T(8,128)(2,1)}, u32[]{:S(2)}, u32[]{:S(2)}) async-start(bf16[64,48,768]{2,1,0:T(8,128)(2,1)} %stack.259), calls=%async_computation | async-start | bytes 9437184 | tf_op jit(solution)/shard_map/all_to_all | solution.py:76
  29.0 0.0 all-gather.3.cloned.1.call-start
  29.1 0.7 all-gather.3.cloned.1.call-update
  29.8 0.0 all-reduce.5.cloned.1.call-start
  29.9 3.5 collective-permute-start
  33.4 1.9 collective-permute-start.1
  35.4 0.0 copy-done.5
  35.4 0.8 broadcast_multiply_fusion
  36.2 0.0 copy-done.9
  36.2 0.2 slice_reduce_fusion.48
  36.4 0.2 slice_reduce_fusion.47
  36.6 0.1 slice_reduce_fusion.46
  36.7 0.0 copy-start.11
  36.7 0.0 copy-start.13
  36.7 0.0 copy-start.15
  36.7 0.0 copy-start.17
  36.7 0.0 copy-start.19
  36.7 228.8 %collective-permute-done = bf16[1,3,64,768]{3,2,1,0:T(8,128)(2,1)S(1)} collective-permute-done((bf16[1,3,64,768]{3,2,1,0:T(8,128)(2,1)S(1)}, bf16[1,3,64,768]{3,2,1,0:T(8,128)(2,1)S(1)}, u32[]{:S(2)}, u32[]{:S(2)}) %collective-permute-start) | collective-permute-done | bytes 294944 | tf_op jit(solution)/shard_map/ppermute | solution.py:18
  265.5 0.1 constant_dynamic-update-slice_fusion
  265.6 2.9 collective-permute-done.1
  268.6 0.3 fusion.12
  268.9 0.0 copy-start.10
  268.9 6.5 fusion.124
  275.4 0.0 copy-done.1
  275.4 0.2 multiply_reduce_fusion.3
  275.7 0.0 copy-done.10
  275.7 0.0 copy-start.21
  275.7 0.9 multiply_convert_fusion.1
  276.6 0.2 all-gather.3.cloned.1.call-done
  276.8 7.6 reshape.400
  284.3 5.5 convolution_add_fusion
  289.9 0.0 all-to-all-done
  289.9 7.3 convert_reduce_fusion
  297.2 1.5 multiply_reduce_fusion.2
  298.7 0.9 copy-done.3
  299.6 0.0 copy-done.22
  299.6 0.9 multiply_reduce_fusion
  300.4 0.6 broadcast_multiply_fusion.1
  301.0 0.7 div.17
  301.7 4.0 fusion.118
  305.7 1.2 fusion.117
  306.9 0.0 copy-start.24
  306.9 0.0 copy-start.23
  306.9 2.0 fusion.119
  308.9 0.0 copy-start.25
  309.0 0.0 copy-start.26
  309.0 0.0 copy-start.6
  309.0 0.0 copy-start.12
  309.0 0.0 copy-start.14
  309.0 0.0 copy-start.16
  309.0 0.0 copy-start.18
  309.6 2.4 collective-permute-start.2
  312.1 2.1 collective-permute-start.3
  314.7 0.0 copy-start.8
  314.7 0.7 copy-done.8
  315.3 0.0 all-reduce.5.cloned.1.call-update
  315.4 107.7 %all-reduce.2 = (f32[768]{0:T(1024)}, f32[3072]{0:T(1024)}) all-reduce(f32[768]{0:T(1024)S(1)} %copy-done.25, f32[3072]{0:T(1024)S(1)} %copy-done.26), channel_id=1, replica_groups=mesh['dp'=8,'tile'=64] {'dp','tile'}, use_global_device_ids=true, to_apply=%region_55.56 | all-reduce | flops 3840 | bytes 30720 | tf_op jit(solution)/shard_map/psum | solution.py:119
  423.1 0.0 collective-permute-done.2
  423.1 0.0 collective-permute-done.3
  423.1 0.3 select_maximum_fusion
  423.5 6.5 fusion.70
  430.0 348.1 %all-reduce.5.cloned.1.call-done = f32[7,7,768]{2,1,0:T(8,128)} async-done(((f32[7,7,768]{2,1,0:T(8,128)}), f32[7,7,768]{2,1,0:T(8,128)}) %all-reduce.5.cloned.1.call-update) | async-done | bytes 150544 | tf_op jit(solution)/shard_map/psum | solution.py:119
  778.1 1.6 copy.21
  (103 shorter events, 0.8 us)
Async XLA Ops:
  10.6 19.3 %copy-start = (bf16[1,4,64,768]{3,2,1,0:T(8,128)(2,1)S(1)}, bf16[1,4,64,768]{3,2,1,0:T(8,128)(2,1)}, u32[]{:S(2)}) copy-start(bf16[1,4,64,768]{3,2,1,0:T(8,128)(2,1)} %param.8) | copy-start | bytes 1179652
  10.6 24.8 %copy-start.27 = (s32[4]{0:T(128)S(1)}, s32[4]{0:T(128)}, u32[]{:S(2)}) copy-start(s32[4]{0:T(128)} %param.15) | copy-start | bytes 52
  10.6 24.8 %copy-start.5 = (bf16[1,4,64,768]{3,2,1,0:T(8,128)(2,1)S(1)}, bf16[1,4,64,768]{3,2,1,0:T(8,128)(2,1)}, u32[]{:S(2)}) copy-start(bf16[1,4,64,768]{3,2,1,0:T(8,128)(2,1)} %param.9) | copy-start | bytes 1179652
  10.6 25.7 %copy-start.9 = (f32[7,7,768]{2,1,0:T(8,128)S(1)}, f32[7,7,768]{2,1,0:T(8,128)}, u32[]{:S(2)}) copy-start(f32[7,7,768]{2,1,0:T(8,128)} %param.10) | copy-start | bytes 451588
  10.6 279.3 %all-to-all-start = ((bf16[64,48,768]{2,1,0:T(8,128)(2,1)}), bf16[64,48,768]{2,1,0:T(8,128)(2,1)}, u32[]{:S(2)}, u32[]{:S(2)}) async-start(bf16[64,48,768]{2,1,0:T(8,128)(2,1)} %stack.259), calls=%async_computation | async-start | bytes 9437184 | tf_op jit(solution)/shard_map/all_to_all | solution.py:76
  29.0 247.7 %all-gather.3.cloned.1.call-start = ((), (), s32[]{:S(2)}) async-start(), calls=%async_computation.2 | async-start | bytes 6389760 | tf_op jit(solution)/shard_map/all_gather | solution.py:74
  29.8 748.3 %all-reduce.5.cloned.1.call-start = ((), (), s32[]{:S(2)}) async-start(), calls=%async_computation.1 | async-start | bytes 344064 | tf_op jit(solution)/shard_map/psum | solution.py:119
  29.9 235.6 %collective-permute-start = (bf16[1,3,64,768]{3,2,1,0:T(8,128)(2,1)S(1)}, bf16[1,3,64,768]{3,2,1,0:T(8,128)(2,1)S(1)}, u32[]{:S(2)}, u32[]{:S(2)}) collective-permute-start(bf16[1,3,64,768]{3,2,1,0:T(8,128)(2,1)S(1)} %get-tuple-element.119), channel_id=1, source_target_pairs={{0,1},{1,2},{2,3},{3,4},{4,5},{5,6},{6,7},{7,8},{8,9},{9,10},{10,1... | collective-permute-start | bytes 884744 | tf_op jit(solution)/shard_map/ppermute | solution.py:18
  33.4 235.1 %collective-permute-start.1 = (bf16[1,3,64,768]{3,2,1,0:T(8,128)(2,1)S(1)}, bf16[1,3,64,768]{3,2,1,0:T(8,128)(2,1)S(1)}, u32[]{:S(2)}, u32[]{:S(2)}) collective-permute-start(bf16[1,3,64,768]{3,2,1,0:T(8,128)(2,1)S(1)} %get-tuple-element.120), channel_id=1, source_target_pairs={{1,0},{2,1},{3,2},{4,3},{5,4},{6,5},{7,6},{8,7},{9,8},{10,9},{11,1... | collective-permute-start | bytes 884744 | tf_op jit(solution)/shard_map/ppermute | solution.py:20
  36.7 232.2 %copy-start.11 = (f32[768]{0:T(1024)}, f32[768]{0:T(1024)S(1)}, u32[]{:S(2)}) copy-start(f32[768]{0:T(1024)S(1)} %get-tuple-element.105) | copy-start | bytes 9220
  36.7 232.2 %copy-start.13 = (f32[768]{0:T(1024)}, f32[768]{0:T(1024)S(1)}, u32[]{:S(2)}) copy-start(f32[768]{0:T(1024)S(1)} %get-tuple-element.106) | copy-start | bytes 9220
  36.7 232.2 %copy-start.15 = (f32[768]{0:T(1024)}, f32[768]{0:T(1024)S(1)}, u32[]{:S(2)}) copy-start(f32[768]{0:T(1024)S(1)} %get-tuple-element.107) | copy-start | bytes 9220
  36.7 232.2 %copy-start.17 = (f32[768]{0:T(1024)}, f32[768]{0:T(1024)S(1)}, u32[]{:S(2)}) copy-start(f32[768]{0:T(1024)S(1)} %get-tuple-element.108) | copy-start | bytes 9220
  36.7 232.2 %copy-start.19 = (f32[768]{0:T(1024)}, f32[768]{0:T(1024)S(1)}, u32[]{:S(2)}) copy-start(f32[768]{0:T(1024)S(1)} %get-tuple-element.109) | copy-start | bytes 9220
  265.6 9.8 %copy-start.1 = (bf16[1,7,64,768]{3,2,1,0:T(8,128)(2,1)}, bf16[1,7,64,768]{3,2,1,0:T(8,128)(2,1)S(1)}, u32[]{:S(2)}) copy-start(bf16[1,7,64,768]{3,2,1,0:T(8,128)(2,1)S(1)} %get-tuple-element.117) | copy-start | bytes 2064388
  268.9 6.7 copy-start.10
  275.7 8.7 %copy-start.21 = (f32[4,64]{1,0:T(4,128)}, f32[4,64]{1,0:T(4,128)S(1)}, u32[]{:S(2)}) copy-start(f32[4,64]{1,0:T(4,128)S(1)} %add_rsqrt_fusion) | copy-start | bytes 3076
  284.3 5.5 copy-start.7
  289.9 7.3 copy-start.4
  297.2 2.4 copy-start.22
  298.7 0.9 copy-start.3
  301.7 4.0 copy-start.2
  306.9 7.7 copy-start.24
  306.9 7.7 copy-start.23
  308.9 6.4 copy-start.25
  309.0 6.4 copy-start.26
  309.0 114.4 %copy-start.6 = (bf16[1,4,64,768]{3,2,1,0:T(8,128)(2,1)S(1)}, bf16[1,4,64,768]{3,2,1,0:T(8,128)(2,1)}, u32[]{:S(2)}) copy-start(bf16[1,4,64,768]{3,2,1,0:T(8,128)(2,1)} %param.9) | copy-start | bytes 1179652
  309.0 114.4 %copy-start.12 = (f32[768]{0:T(1024)S(1)}, f32[768]{0:T(1024)}, u32[]{:S(2)}) copy-start(f32[768]{0:T(1024)} %copy-done.11) | copy-start | bytes 9220
  309.0 114.4 %copy-start.14 = (f32[768]{0:T(1024)S(1)}, f32[768]{0:T(1024)}, u32[]{:S(2)}) copy-start(f32[768]{0:T(1024)} %copy-done.13) | copy-start | bytes 9220
  309.0 114.4 %copy-start.16 = (f32[768]{0:T(1024)S(1)}, f32[768]{0:T(1024)}, u32[]{:S(2)}) copy-start(f32[768]{0:T(1024)} %copy-done.15) | copy-start | bytes 9220
  309.0 114.4 %copy-start.18 = (f32[768]{0:T(1024)S(1)}, f32[768]{0:T(1024)}, u32[]{:S(2)}) copy-start(f32[768]{0:T(1024)} %copy-done.17) | copy-start | bytes 9220
  309.0 114.4 %copy-start.20 = (f32[768]{0:T(1024)S(1)}, f32[768]{0:T(1024)}, u32[]{:S(2)}) copy-start(f32[768]{0:T(1024)} %copy-done.19) | copy-start | bytes 9220
  309.6 113.4 %collective-permute-start.2 = (bf16[1,3,64,768]{3,2,1,0:T(8,128)(2,1)S(1)}, bf16[1,3,64,768]{3,2,1,0:T(8,128)(2,1)S(1)}, u32[]{:S(2)}, u32[]{:S(2)}) collective-permute-start(bf16[1,3,64,768]{3,2,1,0:T(8,128)(2,1)S(1)} %get-tuple-element.115), channel_id=1, source_target_pairs={{0,1},{1,2},{2,3},{3,4},{4,5},{5,6},{6,7},{7,8},{8,9},{9,10},{10,1... | collective-permute-start | bytes 884744 | tf_op jit(solution)/shard_map/ppermute | solution.py:18
  312.1 111.0 %collective-permute-start.3 = (bf16[1,3,64,768]{3,2,1,0:T(8,128)(2,1)S(1)}, bf16[1,3,64,768]{3,2,1,0:T(8,128)(2,1)S(1)}, u32[]{:S(2)}, u32[]{:S(2)}) collective-permute-start(bf16[1,3,64,768]{3,2,1,0:T(8,128)(2,1)S(1)} %get-tuple-element.116), channel_id=1, source_target_pairs={{1,0},{2,1},{3,2},{4,3},{5,4},{6,5},{7,6},{8,7},{9,8},{10,9},{11,1... | collective-permute-start | bytes 884744 | tf_op jit(solution)/shard_map/ppermute | solution.py:20
  314.7 0.7 copy-start.8
Sparse Core Ops, SparseCore 0:
  32.0 244.7 all-gather.2
  315.5 462.5 all-reduce.4
